TPU v7x, 32 devices: a whole 2x2x4 slice. The times are simulated.
32 devices in a mesh: wide: 16 (over z, x, core), narrow: 2 (over y).
Axes of the slice: x: 2, y: 2, z: 4, core: 2. Of those that a mesh axis runs over, the one named last changes fastest.
Arguments:
- query_rows: bfloat16 [640, 6144], P('wide', 'narrow'), may hold values from -30 to 30
- key_rows: bfloat16 [640, 6144], P('wide', 'narrow'), may hold values from -10 to 10
- value_rows: bfloat16 [640, 6144], P('wide', 'narrow'), may hold values from -6 to 6
- mid_grad: bfloat16 [5120, 2048], P(('wide', 'narrow')), may hold values from -6 to 6
- link_weight: bfloat16 [768, 2048], replicated, may hold values from -0.21875 to 0.21875
Outputs:
- query_grad: bfloat16 [640, 6144], P('wide', 'narrow')
- key_grad: bfloat16 [640, 6144], P('wide', 'narrow')
- value_grad: bfloat16 [640, 6144], P('wide', 'narrow')
All inputs are finite; a program needn't handle non-finite values.
Results may differ from a plain program's by a relative error of at most 0.0066.
Values may be sent and summed in bfloat16 or wider, within the bound.
No kernel may reach another device: no remote copies, remote signals or barrier semaphores. Data moves between devices by JAX's collectives and lax.ppermute only.
A program may use at most 64 MiB of HBM per device.

v0:
```python
import math
import jax
import jax.numpy as jnp
from jax import lax
from jax.sharding import PartitionSpec as P

HD = 128
PATCH = 8
lowest = -1e30


def on_device(query_rows, key_rows, value_rows, mid_grad, link_weight):
    groups = lax.axis_size("narrow")
    patches = query_rows.shape[0]
    columns = query_rows.shape[1]
    heads_here = columns // HD
    scaling = 1.0 / math.sqrt(HD)
    local_patches = mid_grad.shape[0] // PATCH
    grouped = mid_grad.reshape(local_patches, groups, PATCH // groups, mid_grad.shape[1])
    moved = jnp.einsum(
        "abcm,pm->abcp",
        lax.all_to_all(grouped, "narrow", split_axis=1, concat_axis=0, tiled=True),
        link_weight,
        preferred_element_type=jnp.float32,
    ).astype(jnp.bfloat16)
    incoming = moved.reshape(patches, columns)
    incoming_heads = incoming.reshape(patches, heads_here, HD)
    query_heads = query_rows.reshape(patches, heads_here, HD)
    key_heads = key_rows.reshape(patches, heads_here, HD)
    value_heads = value_rows.reshape(patches, heads_here, HD)
    own_pos = lax.axis_index("wide") * patches + jnp.arange(patches, dtype=jnp.int32)
    total_rows = patches * lax.axis_size("wide")
    empty_store = jnp.zeros((total_rows, columns), jnp.bfloat16)
    fold_start = (
        jnp.full((heads_here, patches), lowest, jnp.float32),
        jnp.zeros((heads_here, patches), jnp.float32),
        jnp.zeros((heads_here, patches), jnp.float32),
        empty_store,
        empty_store,
    )
    pieces = (
        lax.all_gather(key_rows, "wide", axis=0, tiled=True),
        lax.all_gather(value_rows, "wide", axis=0, tiled=True),
    )
    key_piece, value_piece = pieces
    piece_rows = key_piece.shape[0]
    key_split = key_piece.reshape(piece_rows, heads_here, HD)
    value_split = value_piece.reshape(piece_rows, heads_here, HD)
    piece_pos = jnp.arange(piece_rows, dtype=jnp.int32)
    allowed = piece_pos[None, None, :] <= own_pos[None, :, None]
    scores = (
        jnp.einsum("qhd,khd->hqk", query_heads, key_split, preferred_element_type=jnp.float32)
        * scaling
    )
    scores = jnp.where(allowed, scores, lowest)
    products = jnp.einsum(
        "qhd,khd->hqk", incoming_heads, value_split, preferred_element_type=jnp.float32
    )
    old_max, old_total, old_tilt = fold_start[:3]
    new_max = jnp.maximum(old_max, jnp.max(scores, axis=2))
    expo = jnp.where(allowed, jnp.exp(scores - new_max[:, :, None]), 0.0)
    stats = (new_max, jnp.sum(expo, axis=2), jnp.sum(expo * products, axis=2))
    key_store = pieces[0]
    value_store = pieces[1]
    folded = stats + (key_store, value_store)
    run_max, run_total, run_tilt = (folded[0], folded[1], folded[2])
    log_total = run_max + jnp.log(run_total)
    row_delta = run_tilt / run_total
    key_all = folded[3].reshape(total_rows, heads_here, HD)
    value_all = folded[4].reshape(total_rows, heads_here, HD)
    every_pos = jnp.arange(total_rows, dtype=jnp.int32)
    allowed_q = every_pos[None, None, :] <= own_pos[None, :, None]
    scores_q = (
        jnp.einsum("qhd,khd->hqk", query_heads, key_all, preferred_element_type=jnp.float32)
        * scaling
    )
    products_q = jnp.einsum(
        "qhd,khd->hqk", incoming_heads, value_all, preferred_element_type=jnp.float32
    )
    weights_q = jnp.where(
        allowed_q, jnp.exp(jnp.where(allowed_q, scores_q, lowest) - log_total[:, :, None]), 0.0
    )
    score_grad_q = (weights_q * (products_q - row_delta[:, :, None])).astype(jnp.bfloat16)
    query_accum = jnp.einsum(
        "hqk,khd->qhd", score_grad_q, key_all, preferred_element_type=jnp.float32
    )
    query_grad = (query_accum * scaling).astype(jnp.bfloat16).reshape(patches, columns)
    total_all, delta_all = (
        lax.all_gather(log_total, "wide", axis=1, tiled=True),
        lax.all_gather(row_delta, "wide", axis=1, tiled=True),
    )
    query_piece = lax.all_gather(query_rows, "wide", axis=0, tiled=True)
    grad_piece = lax.all_gather(incoming, "wide", axis=0, tiled=True)
    piece_rows = query_piece.shape[0]
    query_split = query_piece.reshape(piece_rows, heads_here, HD)
    grad_split = grad_piece.reshape(piece_rows, heads_here, HD)
    piece_pos = jnp.arange(piece_rows, dtype=jnp.int32)
    allowed = own_pos[None, None, :] <= piece_pos[None, :, None]
    scores = (
        jnp.einsum("qhd,khd->hqk", query_split, key_heads, preferred_element_type=jnp.float32)
        * scaling
    )
    scores = jnp.where(allowed, scores, lowest)
    products = jnp.einsum(
        "qhd,khd->hqk", grad_split, value_heads, preferred_element_type=jnp.float32
    )
    weights = jnp.where(allowed, jnp.exp(scores - total_all[:, :, None]), 0.0)
    score_grad = (weights * (products - delta_all[:, :, None])).astype(jnp.bfloat16)
    key_accum = jnp.einsum(
        "hqk,qhd->khd", score_grad, query_split, preferred_element_type=jnp.float32
    )
    value_accum = jnp.einsum(
        "hqk,qhd->khd", weights.astype(jnp.bfloat16), grad_split, preferred_element_type=jnp.float32
    )
    key_accum, value_accum = (key_accum, value_accum)
    key_grad = (key_accum * scaling).astype(jnp.bfloat16).reshape(patches, columns)
    value_grad = value_accum.astype(jnp.bfloat16).reshape(patches, columns)
    return (query_grad, key_grad, value_grad)


def solution(mesh):
    in_specs = (
        P("wide", "narrow"),
        P("wide", "narrow"),
        P("wide", "narrow"),
        P(("wide", "narrow"), None),
        P(),
    )
    out_specs = (P("wide", "narrow"), P("wide", "narrow"), P("wide", "narrow"))
    return jax.shard_map(
        on_device, mesh=mesh, in_specs=in_specs, out_specs=out_specs, check_vma=False
    )
```

profile of v0, /device:TPU:0, one launch (start us, length us, event | category | flops | bytes accessed | tf_op | source)
XLA Modules:
  0.0 240.6 jit_solution(15646590345335519802)
XLA Ops:
  7.2 0.0 copy-start
  7.2 0.0 all-gather.7.cloned.1.call-start
  7.2 0.7 all-gather.7.cloned.1.call-update
  7.9 0.0 all-gather.9.cloned.1.call-start
  8.0 0.7 all-gather.9.cloned.1.call-update
  8.7 0.0 all-gather.11.cloned.1.call-start
  8.7 0.7 all-gather.11.cloned.1.call-update
  9.4 0.0 all-gather.13.cloned.1.call-start
  9.4 2.3 reshape.125
  11.7 1.4 copy.35
  13.1 13.4 %all_to_all.15 = bf16[20,2,4,2048]{3,2,0,1:T(4,128)(2,1)S(1)} all-to-all(bf16[20,2,4,2048]{3,2,0,1:T(4,128)(2,1)S(1)} %copy.35), channel_id=1, replica_groups=mesh['wide'=16,'narrow'=2] {'narrow'}, dimensions={1} | all-to-all | bytes 1310720 | tf_op jit(solution)/shard_map/all_to_all | solution.py:22
  26.6 0.0 copy-done
  26.6 1.5 fusion.25
  28.0 0.7 copy.67
  28.8 0.0 all-gather.13.cloned.1.call-update
  28.8 0.1 iota_compare_fusion.1
  28.9 0.1 iota_compare_fusion
  29.0 0.8 copy.37
  29.8 1.7 reshape_reshape.3
  31.5 30.6 %all-gather.7.cloned.1.call-done = bf16[640,3072]{1,0:T(8,128)(2,1)} async-done(((bf16[40,3072]{1,0:T(8,128)(2,1)}), bf16[640,3072]{1,0:T(8,128)(2,1)}) %all-gather.7.cloned.1.call-update) | async-done | bytes 3932176 | tf_op jit(solution)/shard_map/all_gather | solution.py:42
  62.1 6.3 %copy.32 = bf16[640,3072]{0,1:T(8,128)(2,1)} copy(bf16[640,3072]{1,0:T(8,128)(2,1)} %all-gather.7.cloned.1.call-done) | data formatting | bytes 7864320 | tf_op jit(solution)/shard_map/all_gather | solution.py:42
  68.4 0.0 copy-start.3
  68.4 43.6 %all-gather.9.cloned.1.call-done = bf16[640,3072]{1,0:T(8,128)(2,1)} async-done(((bf16[40,3072]{1,0:T(8,128)(2,1)}), bf16[640,3072]{1,0:T(8,128)(2,1)}) %all-gather.9.cloned.1.call-update) | async-done | bytes 3932176 | tf_op jit(solution)/shard_map/all_gather | solution.py:43
  112.0 6.2 %copy.38 = bf16[640,3072]{0,1:T(8,128)(2,1)} copy(bf16[640,3072]{1,0:T(8,128)(2,1)} %all-gather.9.cloned.1.call-done) | data formatting | bytes 7864320 | tf_op jit(solution)/shard_map/all_gather | solution.py:43
  118.3 0.0 copy-done.3
  118.3 0.0 copy-start.2
  118.3 0.0 copy-start.5
  118.3 3.3 %fusion.57 = (f32[24,40]{1,0:T(8,128)S(1)}, f32[24,40,640]{2,1,0:T(8,128)S(1)}) fusion(bf16[640,24,128]{0,2,1:T(8,128)(2,1)} %bitcast.76, pred[40,640]{1,0:T(8,128)(4,1)S(1)} %iota_compare_fusion.1, bf16[40,3072]{1,0:T(8,128)(2,1)S(1)} %copy-done.3), kind=kOutput, calls=%fused_computation.62 | convolution fusion | flops 159128640 | bytes 6664960 | tf_op jit(solution)/shard_map/qhd,khd->hqk/dot_general | solution.py:74
  121.6 0.2 copy-done.2
  121.8 0.0 copy-done.5
  121.8 0.0 copy-start.1
  121.8 1.4 fusion.2
  123.2 0.7 copy-done.1
  123.9 1.8 fusion.33
  125.7 0.7 copy.94
  126.4 19.6 %all-gather = f32[16,40,24]{1,2,0:T(8,128)S(1)} all-gather(f32[1,40,24]{1,2,0:T(8,128)S(1)} %bitcast.88), channel_id=1, replica_groups=mesh['wide'=16,'narrow'=2] {'wide'}, dimensions={0}, use_global_device_ids=true | all-gather | bytes 65280 | tf_op jit(solution)/shard_map/all_gather | solution.py:89
  146.1 0.1 reshape.137
  146.2 18.5 %all-gather.1 = f32[16,40,24]{1,2,0:T(8,128)S(1)} all-gather(f32[1,40,24]{1,2,0:T(8,128)S(1)} %bitcast.87), channel_id=1, replica_groups=mesh['wide'=16,'narrow'=2] {'wide'}, dimensions={0}, use_global_device_ids=true | all-gather | bytes 65280 | tf_op jit(solution)/shard_map/all_gather | solution.py:90
  164.7 0.1 reshape.139
  164.9 0.0 copy-start.4
  164.9 0.0 all-gather.11.cloned.1.call-done
  164.9 6.4 %copy.43 = bf16[640,3072]{0,1:T(8,128)(2,1)} copy(bf16[640,3072]{1,0:T(8,128)(2,1)} %all-gather.11.cloned.1.call-done) | data formatting | bytes 7864320 | tf_op jit(solution)/shard_map/all_gather | solution.py:92
  171.4 0.0 copy-done.4
  171.4 4.5 %fusion.43 = f32[24,640,40]{1,2,0:T(8,128)} fusion(bf16[640,24,128]{0,2,1:T(8,128)(2,1)} %bitcast.78, bf16[40,3072]{1,0:T(8,128)(2,1)S(1)} %copy-done.4), kind=kOutput, calls=%fused_computation.43 | convolution fusion | flops 157286400 | bytes 6635520 | tf_op jit(solution)/shard_map/qhd,khd->hqk/dot_general | solution.py:100
  175.9 37.4 %all-gather.13.cloned.1.call-done = bf16[640,3072]{1,0:T(8,128)(2,1)} async-done(((bf16[40,3072]{1,0:T(8,128)(2,1)}), bf16[640,3072]{1,0:T(8,128)(2,1)}) %all-gather.13.cloned.1.call-update) | async-done | bytes 3932176 | tf_op jit(solution)/shard_map/all_gather | solution.py:93
  213.3 6.3 %copy.48 = bf16[640,3072]{0,1:T(8,128)(2,1)} copy(bf16[640,3072]{1,0:T(8,128)(2,1)} %all-gather.13.cloned.1.call-done) | data formatting | bytes 7864320 | tf_op jit(solution)/shard_map/all_gather | solution.py:93
  219.6 0.0 copy-start.6
  219.6 5.3 %fusion.35 = bf16[24,5,8,128]{3,2,1,0:T(8,128)(2,1)} fusion(bf16[640,24,128]{0,2,1:T(8,128)(2,1)} %bitcast.81, f32[24,640,40]{1,2,0:T(8,128)} %fusion.43, f32[24,640]{1,0:T(8,128)S(1)} %bitcast.89, pred[640,40]{0,1:T(8,128)(4,1)S(1)} %iota_compare_fusion), kind=kOutput, calls=%fused_computation.36 | convolution fusion | flops 160481280 | bytes 6722560 | tf_op jit(solution)/shard_map/hqk,qhd->khd/dot_general | solution.py:112
  224.9 0.0 copy-done.6
  224.9 7.3 %fusion.34 = bf16[24,5,8,128]{3,2,1,0:T(8,128)(2,1)} fusion(bf16[640,24,128]{0,2,1:T(8,128)(2,1)} %bitcast.79, f32[24,640,40]{1,2,0:T(8,128)} %fusion.43, bf16[640,24,128]{0,2,1:T(8,128)(2,1)} %bitcast.82, f32[24,640]{1,0:T(8,128)S(1)} %bitcast.91, f32[24,640]{1,0:T(8,128)S(1)} %bitcast.90, pred[640,40]{0,1:T(8,128)(4,1)S(1)} %iota_compare_fusion, ...), kind=kOutput, calls=%fused_computation.35 | convolution fusion | flops 319119360 | bytes 10961920 | tf_op jit(solution)/shard_map/hqk,qhd->khd/dot_general | solution.py:109
  232.1 1.9 copy_bitcast_fusion
  (5 shorter events, 0.1 us)
Async XLA Ops:
  7.2 19.4 %copy-start = (bf16[768,2048]{1,0:T(8,128)(2,1)S(1)}, bf16[768,2048]{1,0:T(8,128)(2,1)}, u32[]{:S(2)}) copy-start(bf16[768,2048]{1,0:T(8,128)(2,1)} %param.9) | copy-start | bytes 9437188
  7.2 54.9 %all-gather.7.cloned.1.call-start = ((), (), s32[]{:S(2)}) async-start(), calls=%async_computation.1 | async-start | bytes 4177920 | tf_op jit(solution)/shard_map/all_gather | solution.py:42
  7.9 104.1 %all-gather.9.cloned.1.call-start = ((), (), s32[]{:S(2)}) async-start(), calls=%async_computation.2 | async-start | bytes 4177920 | tf_op jit(solution)/shard_map/all_gather | solution.py:43
  8.7 156.2 %all-gather.11.cloned.1.call-start = ((), (), s32[]{:S(2)}) async-start(), calls=%async_computation.3 | async-start | bytes 4177920 | tf_op jit(solution)/shard_map/all_gather | solution.py:92
  9.4 203.9 %all-gather.13.cloned.1.call-start = ((), (), s32[]{:S(2)}) async-start(), calls=%async_computation.4 | async-start | bytes 4177920 | tf_op jit(solution)/shard_map/all_gather | solution.py:93
  68.4 49.9 %copy-start.3 = (bf16[40,3072]{1,0:T(8,128)(2,1)S(1)}, bf16[40,3072]{1,0:T(8,128)(2,1)}, u32[]{:S(2)}) copy-start(bf16[40,3072]{1,0:T(8,128)(2,1)} %param.5) | copy-start | bytes 737284
  118.3 3.5 %copy-start.2 = (bf16[640,3072]{0,1:T(8,128)(2,1)S(1)}, bf16[640,3072]{0,1:T(8,128)(2,1)}, u32[]{:S(2)}) copy-start(bf16[640,3072]{0,1:T(8,128)(2,1)} %copy.38) | copy-start | bytes 11796484
  118.3 3.5 %copy-start.5 = (bf16[40,24,128]{2,1,0:T(8,128)(2,1)S(1)}, bf16[40,24,128]{2,1,0:T(8,128)(2,1)}, u32[]{:S(2)}) copy-start(bf16[40,24,128]{2,1,0:T(8,128)(2,1)} %reshape_reshape.3) | copy-start | bytes 737284
  121.8 2.1 copy-start.1
  164.9 6.5 %copy-start.4 = (bf16[40,3072]{1,0:T(8,128)(2,1)S(1)}, bf16[40,3072]{1,0:T(8,128)(2,1)}, u32[]{:S(2)}) copy-start(bf16[40,3072]{1,0:T(8,128)(2,1)} %param.6) | copy-start | bytes 737284
  219.6 5.3 %copy-start.6 = (bf16[40,3072]{1,0:T(8,128)(2,1)S(1)}, bf16[40,3072]{1,0:T(8,128)(2,1)}, u32[]{:S(2)}) copy-start(bf16[40,3072]{1,0:T(8,128)(2,1)} %param.7) | copy-start | bytes 737284
Sparse Core Ops, SparseCore 0:
  10.3 51.7 all-gather.6
  64.3 47.6 all-gather.8
  114.3 48.4 all-gather.10
  164.9 48.3 all-gather.12
where the time goes:
time: 241 us
  waiting for transfers between devices  114 us (47%)
  blocking collectives  51.5 us (21%)
  local copies, waits for them, and re-layouts  36.1 us (15%)
  matrix products  25 us (10%)
  between operations  13.9 us (6%)
    all_gather x1, waiting for transfers between devices, on_device(): lax.all_gather(value_rows, 'wide', axis=0, tiled=True)  43.6 us
    all_gather x1, waiting for transfers between devices, on_device(): grad_piece = lax.all_gather(incoming, 'wide', axis=0, tiled=True)  37.4 us
    all_gather x1, waiting for transfers between devices, on_device(): lax.all_gather(key_rows, 'wide', axis=0, tiled=True)  30.6 us
    all_gather x1, blocking collectives, on_device(): lax.all_gather(log_total, 'wide', axis=1, tiled=True)  19.6 us
    all_gather x1, blocking collectives, on_device(): lax.all_gather(row_delta, 'wide', axis=1, tiled=True)  18.5 us
    all_to_all x1, blocking collectives, on_device(): lax.all_to_all(grouped, 'narrow', split_axis=1, concat_axis=0, tiled=True)  13.4 us
    dot_general x1, matrix products, on_device(): jnp.einsum('hqk,qhd->khd', score_grad, query_split, preferred_element_typ...  7.27 us
    all_gather x1, local copies, waits for them, and re-layouts, on_device(): query_piece = lax.all_gather(query_rows, 'wide', axis=0, tiled=True)  6.45 us
  transfers between devices with their start and end apart: 4, of which 3 were waited for; matrix products, arithmetic and copies ran while one was open for 16% of the time, Pallas kernels for 0%

commit v1 on v0

--- a/solution.py
+++ b/solution.py
@@ -1,3 +1,4 @@
+import functools
 import math
 import jax
 import jax.numpy as jnp
@@ -7,6 +8,25 @@
 HD = 128
 PATCH = 8
 lowest = -1e30
+
+
+def series_all_set(body, ax_name, dim_at):
+    many = lax.axis_size(ax_name)
+    even = sorted(((tick, (tick + 1) % many) for tick in range(many)))
+    latest = body
+    pages = [latest]
+    pp = 1
+    while pp < many:
+        latest = lax.ppermute(latest, axis_name=ax_name, perm=even)
+        pages.insert(0, latest)
+        pp += 1
+    arr_out = jnp.concatenate(pages, dim_at)
+    x_next = lax.axis_index(ax_name)
+    small = x_next + 1
+    return jnp.roll(arr_out, small * body.shape[dim_at], dim_at)
+
+
+unite_area_here = functools.partial(series_all_set, ax_name="wide", dim_at=0)
 
 
 def on_device(query_rows, key_rows, value_rows, mid_grad, link_weight):
@@ -90,7 +110,7 @@
         lax.all_gather(row_delta, "wide", axis=1, tiled=True),
     )
     query_piece = lax.all_gather(query_rows, "wide", axis=0, tiled=True)
-    grad_piece = lax.all_gather(incoming, "wide", axis=0, tiled=True)
+    grad_piece = unite_area_here(incoming)
     piece_rows = query_piece.shape[0]
     query_split = query_piece.reshape(piece_rows, heads_here, HD)
     grad_split = grad_piece.reshape(piece_rows, heads_here, HD)

time: 241 us -> 301 us (1.25)
  waiting for transfers between devices: 114 us -> 143 us
  local copies, waits for them, and re-layouts: 36.1 us -> 64.5 us
    ppermute x0 -> x15, waiting for transfers between devices: none -> 142 us  [series_all_set(): latest = lax.ppermute(latest, axis_name=ax_name, perm=even)]
    all_gather x1, waiting for transfers between devices: 43.6 us -> 0.01 us  [on_device(): lax.all_gather(value_rows, 'wide', axis=0, tiled=True)]
    all_gather x1 -> x0, waiting for transfers between devices: 37.4 us -> none  [on_device(): grad_piece = lax.all_gather(incoming, 'wide', axis=0, tiled=True)]
    all_gather x1, waiting for transfers between devices: 30.6 us -> 0.01 us  [on_device(): lax.all_gather(key_rows, 'wide', axis=0, tiled=True)]
    unnamed x16 -> x97, local copies, waits for them, and re-layouts: 1.19 us -> 26.5 us
    dynamic_slice x0 -> x2, local copies, waits for them, and re-layouts: none -> 9.27 us  [series_all_set(): return jnp.roll(arr_out, small * body.shape[dim_at], dim_at)]
    all_gather x1 -> x0, local copies, waits for them, and re-layouts: 6.29 us -> none  [on_device(): grad_piece = lax.all_gather(incoming, 'wide', axis=0, tiled=True)]
  transfers between devices with their start and end apart: 4 -> 18, of which waited for: 3 -> 15; matrix products, arithmetic and copies ran while one was open for 16% -> 19% of each run, Pallas kernels for 0% -> 0%
where the time goes in v1:
time: 301 us; the launch traced here: 300 us
  waiting for transfers between devices  143 us (48%)
  local copies, waits for them, and re-layouts  64.5 us (21%)
  blocking collectives  50.9 us (17%)
  matrix products  25.9 us (9%)
  between operations  14.3 us (5%)
    ppermute x15, waiting for transfers between devices, series_all_set(): latest = lax.ppermute(latest, axis_name=ax_name, perm=even)  142 us
    unnamed x97, local copies, waits for them, and re-layouts  26.5 us
    all_gather x1, blocking collectives, on_device(): lax.all_gather(row_delta, 'wide', axis=1, tiled=True)  19.8 us
    all_gather x1, blocking collectives, on_device(): lax.all_gather(log_total, 'wide', axis=1, tiled=True)  17.6 us
    all_to_all x1, blocking collectives, on_device(): lax.all_to_all(grouped, 'narrow', split_axis=1, concat_axis=0, tiled=True)  13.4 us
    dynamic_slice x2, local copies, waits for them, and re-layouts, series_all_set(): return jnp.roll(arr_out, small * body.shape[dim_at], dim_at)  9.27 us
    dot_general x1, matrix products, on_device(): jnp.einsum('hqk,qhd->khd', score_grad, query_split, preferred_element_typ...  7.28 us
    all_gather x1, local copies, waits for them, and re-layouts, on_device(): lax.all_gather(value_rows, 'wide', axis=0, tiled=True)  6.3 us
  transfers between devices with their start and end apart: 18, of which 15 were waited for; matrix products, arithmetic and copies ran while one was open for 19% of the time, Pallas kernels for 0%

profile of v1, /device:TPU:0, one launch (start us, length us, event | category | flops | bytes accessed | tf_op | source)
XLA Modules:
  0.0 300.1 jit_solution(583630859445377734)
XLA Ops:
  8.0 0.7 all-gather.8.cloned.1.call-update
  8.7 2.4 reshape.125
  11.1 1.4 copy.35
  12.5 13.4 %all_to_all.15 = bf16[20,2,4,2048]{3,2,0,1:T(4,128)(2,1)S(1)} all-to-all(bf16[20,2,4,2048]{3,2,0,1:T(4,128)(2,1)S(1)} %copy.35), channel_id=1, replica_groups=mesh['wide'=16,'narrow'=2] {'narrow'}, dimensions={1} | all-to-all | bytes 1310720 | tf_op jit(solution)/shard_map/all_to_all | solution.py:42
  25.9 1.5 fusion.25
  27.5 10.0 %collective-permute-done = bf16[40,3072]{1,0:T(8,128)(2,1)S(1)} collective-permute-done((bf16[40,3072]{1,0:T(8,128)(2,1)S(1)}, bf16[40,3072]{1,0:T(8,128)(2,1)S(1)}, u32[]{:S(2)}, u32[]{:S(2)}) %collective-permute-start) | collective-permute-done | bytes 245792 | tf_op jit(solution)/shard_map/ppermute | solution.py:20
  37.4 0.7 copy-done.5
  38.1 11.5 %collective-permute-done.1 = bf16[40,3072]{1,0:T(8,128)(2,1)S(1)} collective-permute-done((bf16[40,3072]{1,0:T(8,128)(2,1)S(1)}, bf16[40,3072]{1,0:T(8,128)(2,1)S(1)}, u32[]{:S(2)}, u32[]{:S(2)}) %collective-permute-start.1) | collective-permute-done | bytes 245792 | tf_op jit(solution)/shard_map/ppermute | solution.py:20
  49.7 0.7 copy-done.7
  50.4 10.3 %collective-permute-done.2 = bf16[40,3072]{1,0:T(8,128)(2,1)S(1)} collective-permute-done((bf16[40,3072]{1,0:T(8,128)(2,1)S(1)}, bf16[40,3072]{1,0:T(8,128)(2,1)S(1)}, u32[]{:S(2)}, u32[]{:S(2)}) %collective-permute-start.2) | collective-permute-done | bytes 245792 | tf_op jit(solution)/shard_map/ppermute | solution.py:20
  60.6 0.7 copy-done.9
  61.4 8.3 %collective-permute-done.3 = bf16[40,3072]{1,0:T(8,128)(2,1)S(1)} collective-permute-done((bf16[40,3072]{1,0:T(8,128)(2,1)S(1)}, bf16[40,3072]{1,0:T(8,128)(2,1)S(1)}, u32[]{:S(2)}, u32[]{:S(2)}) %collective-permute-start.3) | collective-permute-done | bytes 245792 | tf_op jit(solution)/shard_map/ppermute | solution.py:20
  69.7 0.7 copy-done.11
  70.4 8.4 %collective-permute-done.4 = bf16[40,3072]{1,0:T(8,128)(2,1)S(1)} collective-permute-done((bf16[40,3072]{1,0:T(8,128)(2,1)S(1)}, bf16[40,3072]{1,0:T(8,128)(2,1)S(1)}, u32[]{:S(2)}, u32[]{:S(2)}) %collective-permute-start.4) | collective-permute-done | bytes 245792 | tf_op jit(solution)/shard_map/ppermute | solution.py:20
  78.8 0.7 copy-done.13
  79.5 12.1 %collective-permute-done.5 = bf16[40,3072]{1,0:T(8,128)(2,1)S(1)} collective-permute-done((bf16[40,3072]{1,0:T(8,128)(2,1)S(1)}, bf16[40,3072]{1,0:T(8,128)(2,1)S(1)}, u32[]{:S(2)}, u32[]{:S(2)}) %collective-permute-start.5) | collective-permute-done | bytes 245792 | tf_op jit(solution)/shard_map/ppermute | solution.py:20
  92.3 10.5 %collective-permute-done.6 = bf16[40,3072]{1,0:T(8,128)(2,1)S(1)} collective-permute-done((bf16[40,3072]{1,0:T(8,128)(2,1)S(1)}, bf16[40,3072]{1,0:T(8,128)(2,1)S(1)}, u32[]{:S(2)}, u32[]{:S(2)}) %collective-permute-start.6) | collective-permute-done | bytes 245792 | tf_op jit(solution)/shard_map/ppermute | solution.py:20
  103.5 12.1 %collective-permute-done.7 = bf16[40,3072]{1,0:T(8,128)(2,1)S(1)} collective-permute-done((bf16[40,3072]{1,0:T(8,128)(2,1)S(1)}, bf16[40,3072]{1,0:T(8,128)(2,1)S(1)}, u32[]{:S(2)}, u32[]{:S(2)}) %collective-permute-start.7) | collective-permute-done | bytes 245792 | tf_op jit(solution)/shard_map/ppermute | solution.py:20
  115.6 0.7 copy-done.19
  116.3 8.3 %collective-permute-done.8 = bf16[40,3072]{1,0:T(8,128)(2,1)S(1)} collective-permute-done((bf16[40,3072]{1,0:T(8,128)(2,1)S(1)}, bf16[40,3072]{1,0:T(8,128)(2,1)S(1)}, u32[]{:S(2)}, u32[]{:S(2)}) %collective-permute-start.8) | collective-permute-done | bytes 245792 | tf_op jit(solution)/shard_map/ppermute | solution.py:20
  125.4 7.6 %collective-permute-done.9 = bf16[40,3072]{1,0:T(8,128)(2,1)S(1)} collective-permute-done((bf16[40,3072]{1,0:T(8,128)(2,1)S(1)}, bf16[40,3072]{1,0:T(8,128)(2,1)S(1)}, u32[]{:S(2)}, u32[]{:S(2)}) %collective-permute-start.9) | collective-permute-done | bytes 245792 | tf_op jit(solution)/shard_map/ppermute | solution.py:20
  133.0 0.7 copy-done.24
  133.7 8.3 %collective-permute-done.10 = bf16[40,3072]{1,0:T(8,128)(2,1)S(1)} collective-permute-done((bf16[40,3072]{1,0:T(8,128)(2,1)S(1)}, bf16[40,3072]{1,0:T(8,128)(2,1)S(1)}, u32[]{:S(2)}, u32[]{:S(2)}) %collective-permute-start.10) | collective-permute-done | bytes 245792 | tf_op jit(solution)/shard_map/ppermute | solution.py:20
  142.0 0.7 copy-done.26
  142.7 8.3 %collective-permute-done.11 = bf16[40,3072]{1,0:T(8,128)(2,1)S(1)} collective-permute-done((bf16[40,3072]{1,0:T(8,128)(2,1)S(1)}, bf16[40,3072]{1,0:T(8,128)(2,1)S(1)}, u32[]{:S(2)}, u32[]{:S(2)}) %collective-permute-start.11) | collective-permute-done | bytes 245792 | tf_op jit(solution)/shard_map/ppermute | solution.py:20
  151.0 0.7 copy-done.28
  151.7 8.4 %collective-permute-done.12 = bf16[40,3072]{1,0:T(8,128)(2,1)} collective-permute-done((bf16[40,3072]{1,0:T(8,128)(2,1)S(1)}, bf16[40,3072]{1,0:T(8,128)(2,1)}, u32[]{:S(2)}, u32[]{:S(2)}) %collective-permute-start.12) | collective-permute-done | bytes 245792 | tf_op jit(solution)/shard_map/ppermute | solution.py:20
  160.2 8.6 %collective-permute-done.13 = bf16[40,3072]{1,0:T(8,128)(2,1)} collective-permute-done((bf16[40,3072]{1,0:T(8,128)(2,1)}, bf16[40,3072]{1,0:T(8,128)(2,1)}, u32[]{:S(2)}, u32[]{:S(2)}) %collective-permute-start.13) | collective-permute-done | bytes 245792 | tf_op jit(solution)/shard_map/ppermute | solution.py:20
  169.6 1.7 copy.37
  171.3 1.7 reshape_reshape.3
  173.1 9.3 %collective-permute-done.14 = bf16[40,3072]{1,0:T(8,128)(2,1)} collective-permute-done((bf16[40,3072]{1,0:T(8,128)(2,1)}, bf16[40,3072]{1,0:T(8,128)(2,1)}, u32[]{:S(2)}, u32[]{:S(2)}) %collective-permute-start.14) | collective-permute-done | bytes 245792 | tf_op jit(solution)/shard_map/ppermute | solution.py:20
  182.4 1.0 constant_dynamic-update-slice_fusion.31
  183.4 1.0 constant_dynamic-update-slice_fusion.30
  184.4 1.0 constant_dynamic-update-slice_fusion.29
  185.3 1.0 constant_dynamic-update-slice_fusion.28
  186.3 1.0 constant_dynamic-update-slice_fusion.27
  187.3 1.0 constant_dynamic-update-slice_fusion.26
  188.2 1.1 constant_dynamic-update-slice_fusion.25
  189.3 1.0 constant_dynamic-update-slice_fusion.24
  190.3 1.0 constant_dynamic-update-slice_fusion.23
  191.2 1.0 constant_dynamic-update-slice_fusion.22
  192.2 1.0 constant_dynamic-update-slice_fusion.21
  193.2 1.0 constant_dynamic-update-slice_fusion.20
  194.2 1.0 constant_dynamic-update-slice_fusion.19
  195.1 1.0 constant_dynamic-update-slice_fusion.18
  196.1 1.0 constant_dynamic-update-slice_fusion.17
  197.1 1.0 constant_dynamic-update-slice_fusion.15
  198.1 1.0 constant_dynamic-update-slice_fusion.14
  199.0 1.0 constant_dynamic-update-slice_fusion.13
  200.5 2.9 constant_dynamic-slice_fusion
  203.4 6.4 %copy.48 = bf16[640,3072]{0,1:T(8,128)(2,1)} copy(bf16[640,3072]{1,0:T(8,128)(2,1)} %constant_dynamic-slice_fusion) | data formatting | bytes 7864320 | tf_op jit(solution)/shard_map/jit(_roll_dynamic)/dynamic_slice | solution.py:26
  209.7 6.3 %copy.32 = bf16[640,3072]{0,1:T(8,128)(2,1)} copy(bf16[640,3072]{1,0:T(8,128)(2,1)} %all-gather.6.cloned.1.call-done) | data formatting | bytes 7864320 | tf_op jit(solution)/shard_map/all_gather | solution.py:62
  216.0 6.3 %copy.38 = bf16[640,3072]{0,1:T(8,128)(2,1)} copy(bf16[640,3072]{1,0:T(8,128)(2,1)} %all-gather.8.cloned.1.call-done) | data formatting | bytes 7864320 | tf_op jit(solution)/shard_map/all_gather | solution.py:63
  222.3 3.2 %fusion.57 = (f32[24,40]{1,0:T(8,128)S(1)}, f32[24,40,640]{2,1,0:T(8,128)S(1)}) fusion(bf16[640,24,128]{0,2,1:T(8,128)(2,1)} %bitcast.76, pred[40,640]{1,0:T(8,128)(4,1)S(1)} %iota_compare_fusion.1, bf16[40,3072]{1,0:T(8,128)(2,1)S(1)} %copy-done.3), kind=kOutput, calls=%fused_computation.95 | convolution fusion | flops 159128640 | bytes 6664960 | tf_op jit(solution)/shard_map/qhd,khd->hqk/dot_general | solution.py:94
  225.6 2.5 fusion.2
  228.1 1.8 fusion.33
  230.0 0.7 copy.94
  230.7 6.2 %copy.43 = bf16[640,3072]{0,1:T(8,128)(2,1)} copy(bf16[640,3072]{1,0:T(8,128)(2,1)} %all-gather.10.cloned.1.call-done) | data formatting | bytes 7864320 | tf_op jit(solution)/shard_map/all_gather | solution.py:112
  236.9 4.3 %fusion.43 = f32[24,640,40]{1,2,0:T(8,128)} fusion(bf16[640,24,128]{0,2,1:T(8,128)(2,1)} %bitcast.78, bf16[40,3072]{1,0:T(8,128)(2,1)S(1)} %copy-done.4), kind=kOutput, calls=%fused_computation.43 | convolution fusion | flops 157286400 | bytes 6635520 | tf_op jit(solution)/shard_map/qhd,khd->hqk/dot_general | solution.py:120
  241.2 17.6 %all-gather = f32[16,40,24]{1,2,0:T(8,128)S(1)} all-gather(f32[1,40,24]{1,2,0:T(8,128)S(1)} %bitcast.90), channel_id=1, replica_groups=mesh['wide'=16,'narrow'=2] {'wide'}, dimensions={0}, use_global_device_ids=true | all-gather | bytes 65280 | tf_op jit(solution)/shard_map/all_gather | solution.py:109
  259.0 19.8 %all-gather.1 = f32[16,40,24]{1,2,0:T(8,128)S(1)} all-gather(f32[1,40,24]{1,2,0:T(8,128)S(1)} %bitcast.89), channel_id=1, replica_groups=mesh['wide'=16,'narrow'=2] {'wide'}, dimensions={0}, use_global_device_ids=true | all-gather | bytes 65280 | tf_op jit(solution)/shard_map/all_gather | solution.py:110
  279.1 5.3 %fusion.35 = bf16[24,5,8,128]{3,2,1,0:T(8,128)(2,1)} fusion(bf16[640,24,128]{0,2,1:T(8,128)(2,1)} %bitcast.81, f32[24,640,40]{1,2,0:T(8,128)} %fusion.43, f32[24,640]{1,0:T(8,128)S(1)} %bitcast.91, pred[640,40]{0,1:T(8,128)(4,1)S(1)} %copy-done.31), kind=kOutput, calls=%fused_computation.36 | convolution fusion | flops 160481280 | bytes 6722560 | tf_op jit(solution)/shard_map/hqk,qhd->khd/dot_general | solution.py:132
  284.4 7.3 %fusion.34 = bf16[24,5,8,128]{3,2,1,0:T(8,128)(2,1)} fusion(bf16[640,24,128]{0,2,1:T(8,128)(2,1)} %bitcast.79, f32[24,640,40]{1,2,0:T(8,128)} %fusion.43, bf16[640,24,128]{0,2,1:T(8,128)(2,1)} %bitcast.82, f32[24,640]{1,0:T(8,128)S(1)} %bitcast.93, f32[24,640]{1,0:T(8,128)S(1)} %bitcast.92, pred[640,40]{0,1:T(8,128)(4,1)S(1)} %copy-done.31, ...), kind=kOutput, calls=%fused_computation.35 | convolution fusion | flops 319119360 | bytes 10961920 | tf_op jit(solution)/shard_map/hqk,qhd->khd/dot_general | solution.py:129
  291.7 1.9 copy_bitcast_fusion
  (102 shorter events, 4.6 us)
Async XLA Ops:
  7.2 18.7 %copy-start = (bf16[768,2048]{1,0:T(8,128)(2,1)S(1)}, bf16[768,2048]{1,0:T(8,128)(2,1)}, u32[]{:S(2)}) copy-start(bf16[768,2048]{1,0:T(8,128)(2,1)} %param.9) | copy-start | bytes 9437188
  7.2 202.6 %all-gather.6.cloned.1.call-start = ((), (), s32[]{:S(2)}) async-start(), calls=%async_computation.1 | async-start | bytes 4177920 | tf_op jit(solution)/shard_map/all_gather | solution.py:62
  7.9 208.1 %all-gather.8.cloned.1.call-start = ((), (), s32[]{:S(2)}) async-start(), calls=%async_computation.2 | async-start | bytes 4177920 | tf_op jit(solution)/shard_map/all_gather | solution.py:63
  8.7 222.0 %all-gather.10.cloned.1.call-start = ((), (), s32[]{:S(2)}) async-start(), calls=%async_computation.3 | async-start | bytes 4177920 | tf_op jit(solution)/shard_map/all_gather | solution.py:112
  27.4 97.3 %copy-start.21 = (bf16[40,4,768]{2,0,1:T(8,128)(2,1)}, bf16[40,4,768]{2,0,1:T(8,128)(2,1)S(1)}, u32[]{:S(2)}) copy-start(bf16[40,4,768]{2,0,1:T(8,128)(2,1)S(1)} %fusion.25) | copy-start | bytes 737284
  27.4 10.0 %collective-permute-start = (bf16[40,3072]{1,0:T(8,128)(2,1)S(1)}, bf16[40,3072]{1,0:T(8,128)(2,1)S(1)}, u32[]{:S(2)}, u32[]{:S(2)}) collective-permute-start(bf16[40,3072]{1,0:T(8,128)(2,1)S(1)} %bitcast.83), channel_id=1, source_target_pairs={{0,2},{2,4},{4,6},{6,8},{8,10},{10,12},{12,14},{14,16},{16,18},{18... | collective-permute-start | bytes 737288 | tf_op jit(solution)/shard_map/ppermute | solution.py:20
  37.4 0.7 copy-start.5
  38.1 11.5 %collective-permute-start.1 = (bf16[40,3072]{1,0:T(8,128)(2,1)S(1)}, bf16[40,3072]{1,0:T(8,128)(2,1)S(1)}, u32[]{:S(2)}, u32[]{:S(2)}) collective-permute-start(bf16[40,3072]{1,0:T(8,128)(2,1)S(1)} %collective-permute-done), channel_id=1, source_target_pairs={{0,2},{2,4},{4,6},{6,8},{8,10},{10,12},{12,14},{14,16},{16,18},{18... | collective-permute-start | bytes 737288 | tf_op jit(solution)/shard_map/ppermute | solution.py:20
  49.7 0.7 copy-start.7
  50.4 10.3 %collective-permute-start.2 = (bf16[40,3072]{1,0:T(8,128)(2,1)S(1)}, bf16[40,3072]{1,0:T(8,128)(2,1)S(1)}, u32[]{:S(2)}, u32[]{:S(2)}) collective-permute-start(bf16[40,3072]{1,0:T(8,128)(2,1)S(1)} %collective-permute-done.1), channel_id=1, source_target_pairs={{0,2},{2,4},{4,6},{6,8},{8,10},{10,12},{12,14},{14,16},{16,18},{18... | collective-permute-start | bytes 737288 | tf_op jit(solution)/shard_map/ppermute | solution.py:20
  60.6 0.7 copy-start.9
  61.4 8.3 %collective-permute-start.3 = (bf16[40,3072]{1,0:T(8,128)(2,1)S(1)}, bf16[40,3072]{1,0:T(8,128)(2,1)S(1)}, u32[]{:S(2)}, u32[]{:S(2)}) collective-permute-start(bf16[40,3072]{1,0:T(8,128)(2,1)S(1)} %collective-permute-done.2), channel_id=1, source_target_pairs={{0,2},{2,4},{4,6},{6,8},{8,10},{10,12},{12,14},{14,16},{16,18},{18... | collective-permute-start | bytes 737288 | tf_op jit(solution)/shard_map/ppermute | solution.py:20
  69.7 0.7 copy-start.11
  70.4 8.4 %collective-permute-start.4 = (bf16[40,3072]{1,0:T(8,128)(2,1)S(1)}, bf16[40,3072]{1,0:T(8,128)(2,1)S(1)}, u32[]{:S(2)}, u32[]{:S(2)}) collective-permute-start(bf16[40,3072]{1,0:T(8,128)(2,1)S(1)} %collective-permute-done.3), channel_id=1, source_target_pairs={{0,2},{2,4},{4,6},{6,8},{8,10},{10,12},{12,14},{14,16},{16,18},{18... | collective-permute-start | bytes 737288 | tf_op jit(solution)/shard_map/ppermute | solution.py:20
  78.8 0.7 copy-start.13
  79.5 12.1 %collective-permute-start.5 = (bf16[40,3072]{1,0:T(8,128)(2,1)S(1)}, bf16[40,3072]{1,0:T(8,128)(2,1)S(1)}, u32[]{:S(2)}, u32[]{:S(2)}) collective-permute-start(bf16[40,3072]{1,0:T(8,128)(2,1)S(1)} %collective-permute-done.4), channel_id=1, source_target_pairs={{0,2},{2,4},{4,6},{6,8},{8,10},{10,12},{12,14},{14,16},{16,18},{18... | collective-permute-start | bytes 737288 | tf_op jit(solution)/shard_map/ppermute | solution.py:20
  91.6 0.7 copy-start.15
  92.3 10.5 %collective-permute-start.6 = (bf16[40,3072]{1,0:T(8,128)(2,1)S(1)}, bf16[40,3072]{1,0:T(8,128)(2,1)S(1)}, u32[]{:S(2)}, u32[]{:S(2)}) collective-permute-start(bf16[40,3072]{1,0:T(8,128)(2,1)S(1)} %collective-permute-done.5), channel_id=1, source_target_pairs={{0,2},{2,4},{4,6},{6,8},{8,10},{10,12},{12,14},{14,16},{16,18},{18... | collective-permute-start | bytes 737288 | tf_op jit(solution)/shard_map/ppermute | solution.py:20
  102.8 0.7 copy-start.17
  103.5 12.1 %collective-permute-start.7 = (bf16[40,3072]{1,0:T(8,128)(2,1)S(1)}, bf16[40,3072]{1,0:T(8,128)(2,1)S(1)}, u32[]{:S(2)}, u32[]{:S(2)}) collective-permute-start(bf16[40,3072]{1,0:T(8,128)(2,1)S(1)} %collective-permute-done.6), channel_id=1, source_target_pairs={{0,2},{2,4},{4,6},{6,8},{8,10},{10,12},{12,14},{14,16},{16,18},{18... | collective-permute-start | bytes 737288 | tf_op jit(solution)/shard_map/ppermute | solution.py:20
  115.6 0.7 copy-start.19
  116.3 8.3 %collective-permute-start.8 = (bf16[40,3072]{1,0:T(8,128)(2,1)S(1)}, bf16[40,3072]{1,0:T(8,128)(2,1)S(1)}, u32[]{:S(2)}, u32[]{:S(2)}) collective-permute-start(bf16[40,3072]{1,0:T(8,128)(2,1)S(1)} %collective-permute-done.7), channel_id=1, source_target_pairs={{0,2},{2,4},{4,6},{6,8},{8,10},{10,12},{12,14},{14,16},{16,18},{18... | collective-permute-start | bytes 737288 | tf_op jit(solution)/shard_map/ppermute | solution.py:20
  124.7 0.7 copy-start.22
  124.7 8.3 %collective-permute-start.9 = (bf16[40,3072]{1,0:T(8,128)(2,1)S(1)}, bf16[40,3072]{1,0:T(8,128)(2,1)S(1)}, u32[]{:S(2)}, u32[]{:S(2)}) collective-permute-start(bf16[40,3072]{1,0:T(8,128)(2,1)S(1)} %collective-permute-done.8), channel_id=1, source_target_pairs={{0,2},{2,4},{4,6},{6,8},{8,10},{10,12},{12,14},{14,16},{16,18},{18... | collective-permute-start | bytes 737288 | tf_op jit(solution)/shard_map/ppermute | solution.py:20
  133.0 0.7 copy-start.24
  133.7 8.3 %collective-permute-start.10 = (bf16[40,3072]{1,0:T(8,128)(2,1)S(1)}, bf16[40,3072]{1,0:T(8,128)(2,1)S(1)}, u32[]{:S(2)}, u32[]{:S(2)}) collective-permute-start(bf16[40,3072]{1,0:T(8,128)(2,1)S(1)} %collective-permute-done.9), channel_id=1, source_target_pairs={{0,2},{2,4},{4,6},{6,8},{8,10},{10,12},{12,14},{14,16},{16,18},{18... | collective-permute-start | bytes 737288 | tf_op jit(solution)/shard_map/ppermute | solution.py:20
  142.0 0.7 copy-start.26
  142.7 8.3 %collective-permute-start.11 = (bf16[40,3072]{1,0:T(8,128)(2,1)S(1)}, bf16[40,3072]{1,0:T(8,128)(2,1)S(1)}, u32[]{:S(2)}, u32[]{:S(2)}) collective-permute-start(bf16[40,3072]{1,0:T(8,128)(2,1)S(1)} %collective-permute-done.10), channel_id=1, source_target_pairs={{0,2},{2,4},{4,6},{6,8},{8,10},{10,12},{12,14},{14,16},{16,18},{18... | collective-permute-start | bytes 737288 | tf_op jit(solution)/shard_map/ppermute | solution.py:20
  151.0 0.7 copy-start.28
  151.7 8.4 %collective-permute-start.12 = (bf16[40,3072]{1,0:T(8,128)(2,1)S(1)}, bf16[40,3072]{1,0:T(8,128)(2,1)}, u32[]{:S(2)}, u32[]{:S(2)}) collective-permute-start(bf16[40,3072]{1,0:T(8,128)(2,1)S(1)} %collective-permute-done.11), channel_id=1, source_target_pairs={{0,2},{2,4},{4,6},{6,8},{8,10},{10,12},{12,14},{14,16},{16,18},{18... | collective-permute-start | bytes 737288 | tf_op jit(solution)/shard_map/ppermute | solution.py:20
  160.1 8.6 %collective-permute-start.13 = (bf16[40,3072]{1,0:T(8,128)(2,1)}, bf16[40,3072]{1,0:T(8,128)(2,1)}, u32[]{:S(2)}, u32[]{:S(2)}) collective-permute-start(bf16[40,3072]{1,0:T(8,128)(2,1)} %collective-permute-done.12), channel_id=1, source_target_pairs={{0,2},{2,4},{4,6},{6,8},{8,10},{10,12},{12,14},{14,16},{16,18},{18... | collective-permute-start | bytes 737288 | tf_op jit(solution)/shard_map/ppermute | solution.py:20
  168.8 13.7 %collective-permute-start.14 = (bf16[40,3072]{1,0:T(8,128)(2,1)}, bf16[40,3072]{1,0:T(8,128)(2,1)}, u32[]{:S(2)}, u32[]{:S(2)}) collective-permute-start(bf16[40,3072]{1,0:T(8,128)(2,1)} %collective-permute-done.13), channel_id=1, source_target_pairs={{0,2},{2,4},{4,6},{6,8},{8,10},{10,12},{12,14},{14,16},{16,18},{18... | collective-permute-start | bytes 737288 | tf_op jit(solution)/shard_map/ppermute | solution.py:20
  173.0 27.0 %copy-start.29 = (bf16[40,3072]{1,0:T(8,128)(2,1)S(1)}, bf16[40,3072]{1,0:T(8,128)(2,1)}, u32[]{:S(2)}) copy-start(bf16[40,3072]{1,0:T(8,128)(2,1)} %copy-done.28) | copy-start | bytes 737284
  173.0 27.0 %copy-start.27 = (bf16[40,3072]{1,0:T(8,128)(2,1)S(1)}, bf16[40,3072]{1,0:T(8,128)(2,1)}, u32[]{:S(2)}) copy-start(bf16[40,3072]{1,0:T(8,128)(2,1)} %copy-done.26) | copy-start | bytes 737284
  173.0 27.0 %copy-start.25 = (bf16[40,3072]{1,0:T(8,128)(2,1)S(1)}, bf16[40,3072]{1,0:T(8,128)(2,1)}, u32[]{:S(2)}) copy-start(bf16[40,3072]{1,0:T(8,128)(2,1)} %copy-done.24) | copy-start | bytes 737284
  173.0 27.1 %copy-start.23 = (bf16[40,3072]{1,0:T(8,128)(2,1)S(1)}, bf16[40,3072]{1,0:T(8,128)(2,1)}, u32[]{:S(2)}) copy-start(bf16[40,3072]{1,0:T(8,128)(2,1)} %copy-done.22) | copy-start | bytes 737284
  173.1 27.1 %copy-start.20 = (bf16[40,3072]{1,0:T(8,128)(2,1)S(1)}, bf16[40,3072]{1,0:T(8,128)(2,1)}, u32[]{:S(2)}) copy-start(bf16[40,3072]{1,0:T(8,128)(2,1)} %copy-done.19) | copy-start | bytes 737284
  173.1 27.1 %copy-start.18 = (bf16[40,3072]{1,0:T(8,128)(2,1)S(1)}, bf16[40,3072]{1,0:T(8,128)(2,1)}, u32[]{:S(2)}) copy-start(bf16[40,3072]{1,0:T(8,128)(2,1)} %copy-done.17) | copy-start | bytes 737284
  173.1 27.2 %copy-start.16 = (bf16[40,3072]{1,0:T(8,128)(2,1)S(1)}, bf16[40,3072]{1,0:T(8,128)(2,1)}, u32[]{:S(2)}) copy-start(bf16[40,3072]{1,0:T(8,128)(2,1)} %copy-done.15) | copy-start | bytes 737284
  173.1 27.2 %copy-start.14 = (bf16[40,3072]{1,0:T(8,128)(2,1)S(1)}, bf16[40,3072]{1,0:T(8,128)(2,1)}, u32[]{:S(2)}) copy-start(bf16[40,3072]{1,0:T(8,128)(2,1)} %copy-done.13) | copy-start | bytes 737284
  173.1 27.2 %copy-start.12 = (bf16[40,3072]{1,0:T(8,128)(2,1)S(1)}, bf16[40,3072]{1,0:T(8,128)(2,1)}, u32[]{:S(2)}) copy-start(bf16[40,3072]{1,0:T(8,128)(2,1)} %copy-done.11) | copy-start | bytes 737284
  173.1 27.2 %copy-start.10 = (bf16[40,3072]{1,0:T(8,128)(2,1)S(1)}, bf16[40,3072]{1,0:T(8,128)(2,1)}, u32[]{:S(2)}) copy-start(bf16[40,3072]{1,0:T(8,128)(2,1)} %copy-done.9) | copy-start | bytes 737284
  173.1 27.3 %copy-start.8 = (bf16[40,3072]{1,0:T(8,128)(2,1)S(1)}, bf16[40,3072]{1,0:T(8,128)(2,1)}, u32[]{:S(2)}) copy-start(bf16[40,3072]{1,0:T(8,128)(2,1)} %copy-done.7) | copy-start | bytes 737284
  173.1 27.3 %copy-start.6 = (bf16[40,3072]{1,0:T(8,128)(2,1)S(1)}, bf16[40,3072]{1,0:T(8,128)(2,1)}, u32[]{:S(2)}) copy-start(bf16[40,3072]{1,0:T(8,128)(2,1)} %copy-done.5) | copy-start | bytes 737284
  209.7 12.6 %copy-start.3 = (bf16[40,3072]{1,0:T(8,128)(2,1)S(1)}, bf16[40,3072]{1,0:T(8,128)(2,1)}, u32[]{:S(2)}) copy-start(bf16[40,3072]{1,0:T(8,128)(2,1)} %param.5) | copy-start | bytes 737284
  222.3 3.3 %copy-start.2 = (bf16[640,3072]{0,1:T(8,128)(2,1)S(1)}, bf16[640,3072]{0,1:T(8,128)(2,1)}, u32[]{:S(2)}) copy-start(bf16[640,3072]{0,1:T(8,128)(2,1)} %copy.38) | copy-start | bytes 11796484
  222.3 5.8 %copy-start.1 = (bf16[640,3072]{0,1:T(8,128)(2,1)S(1)}, bf16[640,3072]{0,1:T(8,128)(2,1)}, u32[]{:S(2)}) copy-start(bf16[640,3072]{0,1:T(8,128)(2,1)} %copy.32) | copy-start | bytes 11796484
  228.1 8.8 %copy-start.4 = (bf16[40,3072]{1,0:T(8,128)(2,1)S(1)}, bf16[40,3072]{1,0:T(8,128)(2,1)}, u32[]{:S(2)}) copy-start(bf16[40,3072]{1,0:T(8,128)(2,1)} %param.6) | copy-start | bytes 737284
  230.7 48.4 %copy-start.31 = (pred[640,40]{0,1:T(8,128)(4,1)S(1)}, pred[640,40]{0,1:T(8,128)(4,1)}, u32[]{:S(2)}) copy-start(pred[640,40]{0,1:T(8,128)(4,1)} %iota_compare_fusion) | copy-start | bytes 76804
  279.0 5.4 %copy-start.30 = (bf16[40,3072]{1,0:T(8,128)(2,1)S(1)}, bf16[40,3072]{1,0:T(8,128)(2,1)}, u32[]{:S(2)}) copy-start(bf16[40,3072]{1,0:T(8,128)(2,1)} %param.7) | copy-start | bytes 737284
Sparse Core Ops, SparseCore 0:
  10.3 55.2 all-gather.5
  67.8 52.4 all-gather.7
  160.3 50.8 all-gather.9
